TPU v7x, 32 devices: a whole 2x2x4 slice. The times are simulated.
32 devices in a mesh: dp: 8 (over z, x), tensor: 4 (over y, core).
Axes of the slice: x: 2, y: 2, z: 4, core: 2. Of those that a mesh axis runs over, the one named last changes fastest.
Arguments:
- images_in: bfloat16 [32, 544, 768], P(('dp', 'tensor')), may hold values from -6 to 6
- crop_lengths: int32 [32, 6], P('dp'), may hold values from 1 to 197, 544 in all within a row
- route_index: int32 [32, 272], P('dp'), may hold values from 0 to 543, as said below
- router_weight: bfloat16 [768], replicated, may hold values from -0.21875 to 0.21875
- norm_gain: bfloat16 [2, 2, 768], replicated, may hold values from 0.5 to 1.5
- norm_shift: bfloat16 [2, 2, 768], replicated, may hold values from -1.75 to 1.75
- qkv_weight: bfloat16 [2, 3, 768, 768], P(None, None, None, 'tensor'), may hold values from -0.21875 to 0.21875
- qv_bias: bfloat16 [2, 2, 768], P(None, None, 'tensor'), may hold values from -3 to 3
- out_weight: bfloat16 [2, 768, 768], P(None, 'tensor'), may hold values from -0.75 to 0.75
- out_bias: bfloat16 [2, 768], replicated, may hold values from -1.75 to 1.75
- fc1_weight: bfloat16 [2, 768, 3072], P(None, None, 'tensor'), may hold values from -0.21875 to 0.21875
- fc1_bias: bfloat16 [2, 3072], P(None, 'tensor'), may hold values from -3 to 3
- fc2_weight: bfloat16 [2, 3072, 768], P(None, 'tensor'), may hold values from -0.109375 to 0.109375
- fc2_bias: bfloat16 [2, 768], replicated, may hold values from -1.75 to 1.75
- out_cotangent: bfloat16 [32, 544, 768], P(('dp', 'tensor')), may hold values from -6 to 6
Outputs:
- images_out: bfloat16 [32, 544, 768], P(('dp', 'tensor'))
- input_grad: float32 [32, 544, 768], P(('dp', 'tensor'))
- router_grad: float32 [768], replicated
- gain_grad: float32 [2, 2, 768], replicated
- shift_grad: float32 [2, 2, 768], replicated
- qkv_grad: float32 [2, 3, 768, 768], P(None, None, None, 'tensor')
- qv_bias_grad: float32 [2, 2, 768], P(None, None, 'tensor')
- out_weight_grad: float32 [2, 768, 768], P(None, 'tensor')
- out_bias_grad: float32 [2, 768], replicated
- fc1_grad: float32 [2, 768, 3072], P(None, None, 'tensor')
- fc1_bias_grad: float32 [2, 3072], P(None, 'tensor')
- fc2_grad: float32 [2, 3072, 768], P(None, 'tensor')
- fc2_bias_grad: float32 [2, 768], replicated
Inputs may be any that keep to these rules, and one draw needn't show every extreme that they name: `route_index`: within each image the 272 positions are distinct and ascending.
All inputs are finite; a program needn't handle non-finite values.
Results may differ from a plain program's by a relative error of at most 0.02.
Values may be sent and summed in bfloat16 or wider, within the bound.
A program may use at most 256 MiB of HBM per device.

v0:
```python
import jax
import jax.numpy as jnp
from jax import lax
from jax.sharding import PartitionSpec as P

HEAD_DIM = 64
norm_eps = 1e-06
mask_fill = -1e30
half_root = 0.7071067811865476
inv_root_tau = 0.3989422804014327


def crop_index(lengths, positions):
    bounds = jnp.cumsum(lengths, axis=-1)
    above = positions[:, :, None] >= bounds[:, None, :]
    return jnp.sum(above.astype(jnp.int32), axis=-1)


def norm_rows(inputs, gain_row, shift_row):
    row_mean = jnp.mean(inputs, axis=-1, keepdims=True)
    centred = inputs - row_mean
    inv_std = lax.rsqrt(jnp.mean(centred * centred, axis=-1, keepdims=True) + norm_eps)
    normalised = centred * inv_std
    return (normalised, inv_std, (normalised * gain_row + shift_row).astype(jnp.bfloat16))


def norm_back(gradient, normalised, inv_std, gain_row):
    features = gradient.shape[-1]
    scaled = gradient * gain_row
    inner = jnp.mean(scaled, axis=-1, keepdims=True) + normalised * jnp.mean(
        scaled * normalised, axis=-1, keepdims=True
    )
    gain_part = jnp.sum((gradient * normalised).reshape(-1, features), axis=0)
    shift_part = jnp.sum(gradient.reshape(-1, features), axis=0)
    return (inv_std * (scaled - inner), gain_part, shift_part)


def gelu_value(preact):
    return 0.5 * preact * (1.0 + lax.erf(preact * half_root))


def gelu_slope(preact):
    return 0.5 * (1.0 + lax.erf(preact * half_root)) + preact * inv_root_tau * jnp.exp(
        -0.5 * preact * preact
    )


def block_images(images_all, length):
    per_block = 1
    while per_block * length < 512 and images_all % (2 * per_block) == 0:
        per_block = per_block * 2
    return per_block


def by_blocks(function, arrays, per_block):
    shaped = jax.tree.map(
        lambda item: item.reshape((item.shape[0] // per_block, per_block) + item.shape[1:]), arrays
    )
    result = lax.map(function, shaped)
    return jax.tree.map(
        lambda item: item.reshape((item.shape[0] * item.shape[1],) + item.shape[2:]), result
    )


def masked_scores(queries, key_rows, crops):
    scale = queries.shape[-1] ** (-0.5)
    raw_scores = (
        jnp.einsum("gqhe,gkhe->ghqk", queries, key_rows, preferred_element_type=jnp.float32) * scale
    )
    same_crop = (crops[:, :, None] == crops[:, None, :])[:, None]
    return jnp.where(same_crop, raw_scores, mask_fill)


def attend_block(block_parts):
    queries, key_rows, values, crops = block_parts
    scores = masked_scores(queries, key_rows, crops)
    row_max = jnp.max(scores, axis=-1, keepdims=True)
    exponent = jnp.exp(scores - row_max)
    row_total = jnp.sum(exponent, axis=-1, keepdims=True)
    attn_probs = (exponent / row_total).astype(jnp.bfloat16)
    head_out = jnp.einsum("ghqk,gkhe->gqhe", attn_probs, values, preferred_element_type=jnp.float32)
    return (head_out.astype(jnp.bfloat16), (row_max + jnp.log(row_total))[..., 0])


def attend_back(block_parts):
    queries, key_rows, values, head_grads, log_total, crops = block_parts
    scale = queries.shape[-1] ** (-0.5)
    scores = masked_scores(queries, key_rows, crops)
    attn_probs = jnp.exp(scores - log_total[..., None])
    low_probs = attn_probs.astype(jnp.bfloat16)
    value_grad = jnp.einsum(
        "ghqk,gqhe->gkhe", low_probs, head_grads, preferred_element_type=jnp.float32
    )
    prob_grad = jnp.einsum(
        "gqhe,gkhe->ghqk", head_grads, values, preferred_element_type=jnp.float32
    )
    score_grad = (
        attn_probs * (prob_grad - jnp.sum(attn_probs * prob_grad, axis=-1, keepdims=True))
    ).astype(jnp.bfloat16)
    query_grad = (
        jnp.einsum("ghqk,gkhe->gqhe", score_grad, key_rows, preferred_element_type=jnp.float32)
        * scale
    )
    key_grad = (
        jnp.einsum("ghqk,gqhe->gkhe", score_grad, queries, preferred_element_type=jnp.float32)
        * scale
    )
    return (
        query_grad.astype(jnp.bfloat16),
        key_grad.astype(jnp.bfloat16),
        value_grad.astype(jnp.bfloat16),
    )


def attention_forward(
    inputs, crops_all, gain_row, shift_row, qkv_weights, qv_biases, out_weights, out_biases
):
    normalised, inv_std, normed = norm_rows(inputs, gain_row, shift_row)
    gathered = lax.all_gather(normed, "tensor", axis=0, tiled=True)
    images_all, length, features = gathered.shape
    local_width = qkv_weights.shape[-1]
    head_shape = (images_all, length, local_width // HEAD_DIM, HEAD_DIM)
    projected = jnp.einsum(
        "gld,cde->glce", gathered, qkv_weights, preferred_element_type=jnp.float32
    )
    queries = (projected[:, :, 0] + qv_biases[0]).astype(jnp.bfloat16).reshape(head_shape)
    key_rows = projected[:, :, 1].astype(jnp.bfloat16).reshape(head_shape)
    values = (projected[:, :, 2] + qv_biases[1]).astype(jnp.bfloat16).reshape(head_shape)
    per_block = block_images(images_all, length)
    head_out, log_total = by_blocks(attend_block, (queries, key_rows, values, crops_all), per_block)
    head_out = head_out.reshape(images_all, length, local_width)
    branch = (
        lax.psum_scatter(
            jnp.einsum("gle,ed->gld", head_out, out_weights, preferred_element_type=jnp.float32),
            "tensor",
            scatter_dimension=0,
            tiled=True,
        )
        + out_biases
    )
    out_keep = (head_out, out_weights)
    kept = (normalised, inv_std, gathered, queries, key_rows, values, log_total, out_keep)
    return (branch, kept)


def attention_back(gradient, kept, crops_all, gain_row, qkv_weights):
    normalised, inv_std, gathered, queries, key_rows, values, log_total, out_keep = kept
    own_count, length, features = gradient.shape
    grad_low = gradient.astype(jnp.bfloat16)
    out_bias_part = jnp.sum(grad_low.reshape(-1, features), axis=0, dtype=jnp.float32)
    images_all = queries.shape[0]
    local_width = queries.shape[2] * queries.shape[3]
    head_out, out_weights = out_keep
    grad_all = lax.all_gather(grad_low, "tensor", axis=0, tiled=True)
    out_part = jnp.einsum("gle,gld->ed", head_out, grad_all, preferred_element_type=jnp.float32)
    head_grads = jnp.einsum(
        "gld,ed->gle", grad_all, out_weights, preferred_element_type=jnp.float32
    )
    head_grads = head_grads.astype(jnp.bfloat16).reshape(queries.shape)
    per_block = block_images(images_all, length)
    query_grad, key_grad, value_grad = by_blocks(
        attend_back, (queries, key_rows, values, head_grads, log_total, crops_all), per_block
    )
    qv_part = jnp.stack(
        [
            jnp.sum(query_grad.reshape(-1, local_width), axis=0, dtype=jnp.float32),
            jnp.sum(value_grad.reshape(-1, local_width), axis=0, dtype=jnp.float32),
        ]
    )
    proj_grad = jnp.stack([query_grad, key_grad, value_grad], axis=2).reshape(
        images_all, length, 3, local_width
    )
    qkv_part = jnp.einsum("gld,glce->cde", gathered, proj_grad, preferred_element_type=jnp.float32)
    normed_grad = lax.psum_scatter(
        jnp.einsum(
            "glce,cde->gld", proj_grad, qkv_weights, preferred_element_type=jnp.float32
        ).astype(jnp.bfloat16),
        "tensor",
        scatter_dimension=0,
        tiled=True,
    ).astype(jnp.float32)
    input_part, gain_part, shift_part = norm_back(normed_grad, normalised, inv_std, gain_row)
    return (input_part, (gain_part, shift_part, qkv_part, qv_part, out_part, out_bias_part))


def dense_forward(
    inputs, gain_row, shift_row, first_weights, first_biases, second_weights, second_biases
):
    normalised, inv_std, normed = norm_rows(inputs, gain_row, shift_row)
    full_first, full_first_bias, full_second = (
        lax.all_gather(first_weights, "tensor", axis=1, tiled=True),
        lax.all_gather(first_biases, "tensor", axis=0, tiled=True),
        lax.all_gather(second_weights, "tensor", axis=0, tiled=True),
    )
    preact = (
        jnp.einsum("gld,df->glf", normed, full_first, preferred_element_type=jnp.float32)
        + full_first_bias
    )
    hidden = gelu_value(preact).astype(jnp.bfloat16)
    branch = (
        jnp.einsum("glf,fd->gld", hidden, full_second, preferred_element_type=jnp.float32)
        + second_biases
    )
    kept = (normalised, inv_std, normed, preact, hidden, full_first, full_second)
    return (branch, kept)


def dense_back(gradient, kept, gain_row):
    normalised, inv_std, normed, preact, hidden, first_weights, second_weights = kept
    own_count, length, features = gradient.shape
    grad_low = gradient.astype(jnp.bfloat16)
    second_bias_part = jnp.sum(grad_low.reshape(-1, features), axis=0, dtype=jnp.float32)
    second_part = jnp.einsum("glf,gld->fd", hidden, grad_low, preferred_element_type=jnp.float32)
    hidden_grad = jnp.einsum(
        "gld,fd->glf", grad_low, second_weights, preferred_element_type=jnp.float32
    )
    pre_grad = (hidden_grad * gelu_slope(preact)).astype(jnp.bfloat16)
    first_bias_part = jnp.sum(pre_grad.reshape(-1, pre_grad.shape[-1]), axis=0, dtype=jnp.float32)
    first_part = jnp.einsum("gld,glf->df", normed, pre_grad, preferred_element_type=jnp.float32)
    normed_grad = jnp.einsum(
        "glf,df->gld", pre_grad, first_weights, preferred_element_type=jnp.float32
    )
    first_part, first_bias_part, second_part = (
        lax.psum_scatter(
            first_part.astype(jnp.bfloat16), "tensor", scatter_dimension=1, tiled=True
        ).astype(jnp.float32),
        lax.psum_scatter(
            first_bias_part.astype(jnp.bfloat16), "tensor", scatter_dimension=0, tiled=True
        ).astype(jnp.float32),
        lax.psum_scatter(
            second_part.astype(jnp.bfloat16), "tensor", scatter_dimension=0, tiled=True
        ).astype(jnp.float32),
    )
    input_part, gain_part, shift_part = norm_back(normed_grad, normalised, inv_std, gain_row)
    return (
        input_part,
        (gain_part, shift_part, first_part, first_bias_part, second_part, second_bias_part),
    )


def body(
    images_in,
    crop_lengths,
    route_index,
    router_weight,
    norm_gain,
    norm_shift,
    qkv_weight,
    qv_bias,
    out_weight,
    out_bias,
    fc1_weight,
    fc1_bias,
    fc2_weight,
    fc2_bias,
    out_cotangent,
):
    own_count, length, features = images_in.shape
    images_all = crop_lengths.shape[0]
    offset = lax.axis_index("tensor") * own_count
    positions = jnp.broadcast_to(jnp.arange(length, dtype=jnp.int32), (images_all, length))
    crops_full = crop_index(crop_lengths, positions)
    crops_chosen = jnp.take_along_axis(crops_full, route_index, axis=1)
    own_index = lax.dynamic_slice_in_dim(route_index, offset, own_count, 0)
    row_index = jnp.arange(own_count, dtype=jnp.int32)[:, None]
    chosen = images_in[row_index, own_index]
    chosen_data = chosen.astype(jnp.float32)
    router_data = router_weight.astype(jnp.float32)
    router_logit = jnp.einsum(
        "nsd,d->ns", chosen, router_weight, preferred_element_type=jnp.float32
    )
    route_rate = 1.0 / (1.0 + jnp.exp(-router_logit))
    attn_one, kept_one = attention_forward(
        chosen_data,
        crops_chosen,
        norm_gain[0, 0],
        norm_shift[0, 0],
        qkv_weight[0],
        qv_bias[0],
        out_weight[0],
        out_bias[0],
    )
    middle = chosen_data + attn_one
    ffn_one, kept_two = dense_forward(
        middle,
        norm_gain[0, 1],
        norm_shift[0, 1],
        fc1_weight[0],
        fc1_bias[0],
        fc2_weight[0],
        fc2_bias[0],
    )
    branches = attn_one + ffn_one
    routed = (
        images_in.astype(jnp.float32)
        .at[row_index, own_index]
        .add(route_rate[:, :, None] * branches)
    )
    attn_two, kept_three = attention_forward(
        routed,
        crops_full,
        norm_gain[1, 0],
        norm_shift[1, 0],
        qkv_weight[1],
        qv_bias[1],
        out_weight[1],
        out_bias[1],
    )
    after_attn = routed + attn_two
    ffn_two, kept_four = dense_forward(
        after_attn,
        norm_gain[1, 1],
        norm_shift[1, 1],
        fc1_weight[1],
        fc1_bias[1],
        fc2_weight[1],
        fc2_bias[1],
    )
    images_out = (after_attn + ffn_two).astype(jnp.bfloat16)
    cotangent = out_cotangent.astype(jnp.float32)
    back_four, grads_four = dense_back(cotangent, kept_four, norm_gain[1, 1])
    grad_after = cotangent + back_four
    back_three, grads_three = attention_back(
        grad_after, kept_three, crops_full, norm_gain[1, 0], qkv_weight[1]
    )
    grad_routed = grad_after + back_three
    grad_chosen = grad_routed[row_index, own_index]
    logit_grad = jnp.sum(grad_chosen * branches, axis=-1) * route_rate * (1.0 - route_rate)
    router_part = jnp.einsum("nsd,ns->d", chosen_data, logit_grad, precision=lax.Precision.HIGHEST)
    branch_grad = route_rate[:, :, None] * grad_chosen
    back_two, grads_two = dense_back(branch_grad, kept_two, norm_gain[0, 1])
    back_one, grads_one = attention_back(
        branch_grad + back_two, kept_one, crops_chosen, norm_gain[0, 0], qkv_weight[0]
    )
    own_grad = logit_grad[:, :, None] * router_data + back_two + back_one
    input_grad = grad_routed.at[row_index, own_index].add(own_grad)
    gain_part = jnp.stack(
        [jnp.stack([grads_one[0], grads_two[0]]), jnp.stack([grads_three[0], grads_four[0]])]
    )
    shift_part = jnp.stack(
        [jnp.stack([grads_one[1], grads_two[1]]), jnp.stack([grads_three[1], grads_four[1]])]
    )
    out_bias_part = jnp.stack([grads_one[5], grads_three[5]])
    second_bias_part = jnp.stack([grads_two[5], grads_four[5]])
    shared = lax.psum(
        (router_part, gain_part, shift_part, out_bias_part, second_bias_part), ("dp", "tensor")
    )
    qkv_part = jnp.stack([grads_one[2], grads_three[2]])
    qv_part = jnp.stack([grads_one[3], grads_three[3]])
    out_part = jnp.stack([grads_one[4], grads_three[4]])
    first_part = jnp.stack([grads_two[2], grads_four[2]])
    first_bias_part = jnp.stack([grads_two[3], grads_four[3]])
    second_part = jnp.stack([grads_two[4], grads_four[4]])
    split = (
        lax.psum(qkv_part.astype(jnp.bfloat16), "dp").astype(jnp.float32),
        lax.psum(qv_part.astype(jnp.bfloat16), "dp").astype(jnp.float32),
        lax.psum(out_part.astype(jnp.bfloat16), "dp").astype(jnp.float32),
        lax.psum(first_part.astype(jnp.bfloat16), "dp").astype(jnp.float32),
        lax.psum(first_bias_part.astype(jnp.bfloat16), "dp").astype(jnp.float32),
        lax.psum(second_part.astype(jnp.bfloat16), "dp").astype(jnp.float32),
    )
    return (
        images_out,
        input_grad,
        shared[0],
        shared[1],
        shared[2],
        split[0],
        split[1],
        split[2],
        shared[3],
        split[3],
        split[4],
        split[5],
        shared[4],
    )


def solution(mesh):
    in_specs = (
        P(("dp", "tensor"), None, None),
        P("dp", None),
        P("dp", None),
        P(),
        P(),
        P(),
        P(None, None, None, "tensor"),
        P(None, None, "tensor"),
        P(None, "tensor", None),
        P(),
        P(None, None, "tensor"),
        P(None, "tensor"),
        P(None, "tensor", None),
        P(),
        P(("dp", "tensor"), None, None),
    )
    out_specs = (
        P(("dp", "tensor"), None, None),
        P(("dp", "tensor"), None, None),
        P(),
        P(),
        P(),
        P(None, None, None, "tensor"),
        P(None, None, "tensor"),
        P(None, "tensor", None),
        P(),
        P(None, None, "tensor"),
        P(None, "tensor"),
        P(None, "tensor", None),
        P(),
    )
    return jax.shard_map(body, mesh=mesh, in_specs=in_specs, out_specs=out_specs, check_vma=False)
```

profile of v0, /device:TPU:0, one launch (start us, length us, event | category | flops | bytes accessed | tf_op | source)
XLA Modules:
  0.0 1083.5 jit_solution(4589102543825514392)
XLA Ops:
  8.0 13.7 %gather_fusion = bf16[272,768]{1,0:T(8,128)(2,1)S(1)} fusion(bf16[1,544,768]{2,1,0:T(8,128)(2,1)} %param.23, s32[272]{0:T(512)S(1)} %get-tuple-element.320), kind=kCustom, calls=%fused_computation | custom fusion | bytes 837760 | tf_op jit(solution)/shard_map/gather | solution.py:266
  24.1 9.3 gather_fusion.2
  33.6 12.8 %all-gather.15.cloned.1.call-done = bf16[4,272,768]{2,1,0:T(8,128)(2,1)} async-done(((bf16[1,272,768]{2,1,0:T(8,128)(2,1)}), bf16[4,272,768]{2,1,0:T(8,128)(2,1)}) %all-gather.15.cloned.1.call-update) | async-done | bytes 1671184 | tf_op jit(solution)/shard_map/all_gather | solution.py:119
  76.7 25.8 %reduce-scatter.9.cloned.1.call-done = f32[1,272,768]{2,1,0:T(8,128)} async-done(((f32[4,272,768]{2,1,0:T(8,128)}), f32[1,272,768]{2,1,0:T(8,128)}) %reduce-scatter.9.cloned.1.call-update) | async-done | bytes 835600 | tf_op jit(solution)/shard_map/reduce_scatter | solution.py:133
  104.1 38.0 %all-gather.23.cloned.1.call-done = bf16[1,768,3072]{2,1,0:T(8,128)(2,1)} async-done(((bf16[1,768,768]{2,1,0:T(8,128)(2,1)}), bf16[1,768,3072]{2,1,0:T(8,128)(2,1)}) %all-gather.23.cloned.1.call-update) | async-done | bytes 4718608 | tf_op jit(solution)/shard_map/all_gather | solution.py:191
  148.3 33.4 %all-gather.25.cloned.1.call-done = bf16[1,3072,768]{2,1,0:T(8,128)(2,1)} async-done(((bf16[1,768,768]{2,1,0:T(8,128)(2,1)}), bf16[1,3072,768]{2,1,0:T(8,128)(2,1)}) %all-gather.25.cloned.1.call-update) | async-done | bytes 4718608 | tf_op jit(solution)/shard_map/all_gather | solution.py:193
  191.6 29.4 %all-gather.17.cloned.1.call-done = bf16[4,544,768]{2,1,0:T(8,128)(2,1)} async-done(((bf16[1,544,768]{2,1,0:T(8,128)(2,1)}), bf16[4,544,768]{2,1,0:T(8,128)(2,1)}) %all-gather.17.cloned.1.call-update) | async-done | bytes 3342352 | tf_op jit(solution)/shard_map/all_gather | solution.py:119
  229.4 25.0 %while.53 = (s32[]{:T(128)}, bf16[4,1,544,3,64]{2,4,3,1,0:T(8,128)(2,1)}, f32[4,1,3,544]{3,2,1,0:T(4,128)S(1)}, bf16[4,1,544,3,64]{2,4,3,1,0:T(8,128)(2,1)}, s32...) while((s32[]{:T(128)}, ...), condition=%wide.region_17.18_spmd, body=%wide.region_14.17_spmd.sunk | while | flops 238331296 | bytes 12944741 | solution.py:59
  266.4 54.2 %reduce-scatter.11.cloned.1.call-done = f32[1,544,768]{2,1,0:T(8,128)} async-done(((f32[4,544,768]{2,1,0:T(8,128)}), f32[1,544,768]{2,1,0:T(8,128)}) %reduce-scatter.11.cloned.1.call-update) | async-done | bytes 1671184 | tf_op jit(solution)/shard_map/reduce_scatter | solution.py:133
  323.9 36.4 %all-gather.27.cloned.1.call-done = bf16[1,768,3072]{2,1,0:T(8,128)(2,1)} async-done(((bf16[1,768,768]{2,1,0:T(8,128)(2,1)}), bf16[1,768,3072]{2,1,0:T(8,128)(2,1)}) %all-gather.27.cloned.1.call-update) | async-done | bytes 4718608 | tf_op jit(solution)/shard_map/all_gather | solution.py:191
  360.3 8.7 multiply_convert_fusion.2
  368.9 31.0 %all-gather.29.cloned.1.call-done = bf16[1,3072,768]{2,1,0:T(8,128)(2,1)} async-done(((bf16[1,768,768]{2,1,0:T(8,128)(2,1)}), bf16[1,3072,768]{2,1,0:T(8,128)(2,1)}) %all-gather.29.cloned.1.call-update) | async-done | bytes 4718608 | tf_op jit(solution)/shard_map/all_gather | solution.py:193
  399.9 8.4 fusion.275
  415.9 29.4 %all-gather.19.cloned.1.call-done = bf16[4,544,768]{2,1,0:T(8,128)(2,1)} async-done(((bf16[1,544,768]{2,1,0:T(8,128)(2,1)}), bf16[4,544,768]{2,1,0:T(8,128)(2,1)}) %all-gather.19.cloned.1.call-update) | async-done | bytes 3342352 | tf_op jit(solution)/shard_map/all_gather | solution.py:154
  452.7 45.8 %while.54 = (s32[]{:T(128)}, bf16[4,1,544,3,64]{2,4,3,1,0:T(8,128)(2,1)}, bf16[4,1,544,3,64]{2,4,3,1,0:T(8,128)(2,1)}, bf16[4,1,544,3,64]{2,4,3,1,0:T(8,128)(2,1...) while((s32[]{:T(128)}, ...), condition=%wide.region_25.26_spmd, body=%wide.region_23.25_spmd.sunk | while | flops 582330752 | bytes 35354008 | solution.py:59
  505.4 39.1 %reduce-scatter.13.cloned.1.call-done = bf16[1,544,768]{2,1,0:T(8,128)(2,1)} async-done(((bf16[4,544,768]{2,1,0:T(8,128)(2,1)}), bf16[1,544,768]{2,1,0:T(8,128)(2,1)}) %reduce-scatter.13.cloned.1.call-update) | async-done | bytes 835600 | tf_op jit(solution)/shard_map/reduce_scatter | solution.py:174
  608.3 13.0 %while.55 = (s32[]{:T(128)}, bf16[2,2,272,3,64]{2,4,3,1,0:T(8,128)(2,1)}, bf16[2,2,272,3,64]{2,4,3,1,0:T(8,128)(2,1)}, bf16[2,2,272,3,64]{2,4,3,1,0:T(8,128)(2,1...) while((s32[]{:T(128)}, ...), condition=%wide.region_34.35_spmd, body=%wide.region_32.34_spmd.sunk | while | flops 288762272 | bytes 28893860 | solution.py:59
  641.2 49.9 %reduce-scatter.17.cloned.1.call-done = bf16[768,768]{1,0:T(8,128)(2,1)} async-done(((bf16[768,3072]{1,0:T(8,128)(2,1)}), bf16[768,768]{1,0:T(8,128)(2,1)}) %reduce-scatter.17.cloned.1.call-update) | async-done | bytes 1179664 | tf_op jit(solution)/shard_map/reduce_scatter | solution.py:224
  694.4 47.2 %reduce-scatter.23.cloned.1.call-done = bf16[768,768]{1,0:T(8,128)(2,1)} async-done(((bf16[3072,768]{1,0:T(8,128)(2,1)}), bf16[768,768]{1,0:T(8,128)(2,1)}) %reduce-scatter.23.cloned.1.call-update) | async-done | bytes 1179664 | tf_op jit(solution)/shard_map/reduce_scatter | solution.py:230
  741.6 50.3 %reduce-scatter.21.cloned.1.call-done = bf16[768,768]{1,0:T(8,128)(2,1)} async-done(((bf16[3072,768]{1,0:T(8,128)(2,1)}), bf16[768,768]{1,0:T(8,128)(2,1)}) %reduce-scatter.21.cloned.1.call-update) | async-done | bytes 1179664 | tf_op jit(solution)/shard_map/reduce_scatter | solution.py:230
  821.5 11.3 %all-reduce.6 = (bf16[3072]{0:T(1024)(128)(2,1)}, bf16[3072]{0:T(1024)(128)(2,1)}) all-reduce(bf16[3072]{0:T(1024)(128)(2,1)} %get-tuple-element.443, bf16[3072]{0:T(1024)(128)(2,1)} %get-tuple-element.445), channel_id=15, replica_groups=mesh['dp'=8,'tensor'=4] {'tensor'}, use_global_device_ids=true, to_apply=%region_66.67.clone | all-reduce | flops 6144 | bytes 24576
  846.5 23.4 %all-reduce.4 = (bf16[2,2,192]{2,1,0:T(2,128)(2,1)S(1)}, bf16[2,768]{1,0:T(2,128)(2,1)S(1)}) all-reduce(bf16[2,2,192]{2,1,0:T(2,128)(2,1)S(1)} %pad_maximum_fusion.15, bf16[2,768]{1,0:T(2,128)(2,1)} %pad_maximum_fusion.14), channel_id=1, replica_groups=mesh['dp'=8,'tensor'=4] {'dp'}, use_global_device_ids=true, to_apply=%region_55.56 | all-reduce | flops 2304 | bytes 9216 | tf_op jit(solution)/shard_map/psum | solution.py:356
  877.2 41.6 %all-reduce.3 = (f32[768]{0:T(1024)}, f32[2,2,768]{2,1,0:T(2,128)}, f32[2,2,768]{2,1,0:T(2,128)}, f32[2,768]{1,0:T(2,128)}, f32[2,768]{1,0:T(2,128)}) all-reduce(f32[768]{0:T(1024)S(1)} %copy-done.82, f32[2,2,768]{2,1,0:T(2,128)S(1)} %pad_maximum_fusion.10, ...), channel_id=1, replica_groups=mesh['dp'=8,'tensor'=4] {'dp','tensor'}, use_global_device_ids=true, to_apply=%region_39.40 | all-reduce | flops 9984 | bytes 79872 | tf_op jit(solution)/shard_map/psum | solution.py:345
  918.8 147.8 %all-reduce.9.cloned.1.call-done = (bf16[2,3,768,192]{2,3,1,0:T(8,128)(2,1)}, bf16[2,192,768]{2,1,0:T(8,128)(2,1)}, bf16[2,768,768]{2,1,0:T(8,128)(2,1)}, bf16[2,768,768]{2,1,0:T(8,128)(2,1)}) async-done(((bf16[2,3,768,192]{2,3,1,0:T(8,128)(2,1)}, bf16[2,192,768]{2,1,0:T(8,128)(2,1)}, bf16[2,768,768]{2,1,0:T(8,128)(2,1)}, bf16[2,768,768]{2,1,0:T(8,128)(2,1)}), (bf16[2,3,768,192]{2,3,1,0:T(8,128)(2,1)}, ...) | async-done | bytes 7077904 | tf_op jit(solution)/shard_map/psum | solution.py:355
  (527 shorter events, 330.3 us)
Async XLA Ops:
  7.2 39.3 %all-gather.15.cloned.1.call-start = ((), (), s32[]{:S(2)}) async-start(), calls=%async_computation.8 | async-start | bytes 2088960 | tf_op jit(solution)/shard_map/all_gather | solution.py:119
  8.0 178.3 %copy-start.97 = (s32[272]{0:T(512)}, s32[272]{0:T(512)S(1)}, u32[]{:S(2)}) copy-start(s32[272]{0:T(512)S(1)} %get-tuple-element.321) | copy-start | bytes 3268
  21.8 80.7 %copy-start.7 = (bf16[272,768]{1,0:T(8,128)(2,1)}, bf16[272,768]{1,0:T(8,128)(2,1)S(1)}, u32[]{:S(2)}) copy-start(bf16[272,768]{1,0:T(8,128)(2,1)S(1)} %gather_fusion) | copy-start | bytes 1253380
  22.3 119.8 %copy-start.60 = (f32[768]{0:T(1024)}, f32[768]{0:T(1024)S(1)}, u32[]{:S(2)}) copy-start(f32[768]{0:T(1024)S(1)} %get-tuple-element.449) | copy-start | bytes 9220
  22.4 119.8 %copy-start.93 = (f32[768]{0:T(1024)}, f32[768]{0:T(1024)S(1)}, u32[]{:S(2)}) copy-start(f32[768]{0:T(1024)S(1)} %get-tuple-element.313) | copy-start | bytes 9220
  23.4 79.0 %reduce-scatter.9.cloned.1.call-start = ((), (), s32[]{:S(2)}) async-start(), calls=%async_computation.9 | async-start | bytes 4177920 | tf_op jit(solution)/shard_map/reduce_scatter | solution.py:133
  63.2 79.0 %all-gather.23.cloned.1.call-start = ((), (), s32[]{:S(2)}) async-start(), calls=%async_computation.20 | async-start | bytes 5898240 | tf_op jit(solution)/shard_map/all_gather | solution.py:191
  66.5 115.2 %all-gather.25.cloned.1.call-start = ((), (), s32[]{:S(2)}) async-start(), calls=%async_computation.21 | async-start | bytes 5898240 | tf_op jit(solution)/shard_map/all_gather | solution.py:193
  69.9 151.1 %all-gather.17.cloned.1.call-start = ((), (), s32[]{:S(2)}) async-start(), calls=%async_computation.10 | async-start | bytes 4177920 | tf_op jit(solution)/shard_map/all_gather | solution.py:119
  76.6 109.7 %copy-start.68 = (f32[272]{0:T(512)}, f32[272]{0:T(512)S(1)}, u32[]{:S(2)}) copy-start(f32[272]{0:T(512)S(1)} %add_divide_fusion) | copy-start | bytes 3268
  191.2 129.5 %reduce-scatter.11.cloned.1.call-start = ((), (), s32[]{:S(2)}) async-start(), calls=%async_computation.11 | async-start | bytes 8355840 | tf_op jit(solution)/shard_map/reduce_scatter | solution.py:133
  259.5 100.8 %all-gather.27.cloned.1.call-start = ((), (), s32[]{:S(2)}) async-start(), calls=%async_computation.22 | async-start | bytes 5898240 | tf_op jit(solution)/shard_map/all_gather | solution.py:191
  260.3 139.7 %all-gather.29.cloned.1.call-start = ((), (), s32[]{:S(2)}) async-start(), calls=%async_computation.23 | async-start | bytes 5898240 | tf_op jit(solution)/shard_map/all_gather | solution.py:193
  261.0 184.3 %all-gather.19.cloned.1.call-start = ((), (), s32[]{:S(2)}) async-start(), calls=%async_computation.12 | async-start | bytes 4177920 | tf_op jit(solution)/shard_map/all_gather | solution.py:154
  415.5 129.1 %reduce-scatter.13.cloned.1.call-start = ((), (), s32[]{:S(2)}) async-start(), calls=%async_computation.13 | async-start | bytes 4177920 | tf_op jit(solution)/shard_map/reduce_scatter | solution.py:174
  505.2 94.7 %all-gather.21.cloned.1.call-start = ((), (), s32[]{:S(2)}) async-start(), calls=%async_computation.14 | async-start | bytes 2088960 | tf_op jit(solution)/shard_map/all_gather | solution.py:154
  568.8 72.4 %reduce-scatter.19.cloned.1.call-start = ((), (), s32[]{:S(2)}) async-start(), calls=%async_computation.17 | async-start | bytes 5898240 | tf_op jit(solution)/shard_map/reduce_scatter | solution.py:224
  576.6 114.5 %reduce-scatter.17.cloned.1.call-start = ((), (), s32[]{:S(2)}) async-start(), calls=%async_computation.16 | async-start | bytes 5898240 | tf_op jit(solution)/shard_map/reduce_scatter | solution.py:224
  583.7 157.9 %reduce-scatter.23.cloned.1.call-start = ((), (), s32[]{:S(2)}) async-start(), calls=%async_computation.19 | async-start | bytes 5898240 | tf_op jit(solution)/shard_map/reduce_scatter | solution.py:230
  592.5 199.3 %reduce-scatter.21.cloned.1.call-start = ((), (), s32[]{:S(2)}) async-start(), calls=%async_computation.18 | async-start | bytes 5898240 | tf_op jit(solution)/shard_map/reduce_scatter | solution.py:230
  599.8 271.3 %reduce-scatter.15.cloned.1.call-start = ((), (), s32[]{:S(2)}) async-start(), calls=%async_computation.15 | async-start | bytes 2088960 | tf_op jit(solution)/shard_map/reduce_scatter | solution.py:174
  629.5 437.1 %all-reduce.9.cloned.1.call-start = ((), (), s32[]{:S(2)}) async-start(), calls=%async_computation.24 | async-start | bytes 14155776 | tf_op jit(solution)/shard_map/psum | solution.py:355
  808.2 64.6 %copy-start.16 = (f32[1,272,768]{2,1,0:T(8,128)S(1)}, f32[1,272,768]{2,1,0:T(8,128)}, u32[]{:S(2)}) copy-start(f32[1,272,768]{2,1,0:T(8,128)} %copy-done.13) | copy-start | bytes 2506756
  877.1 193.2 %copy-start.4 = (f32[544,768]{1,0:T(8,128)}, f32[544,768]{1,0:T(8,128)S(1)}, u32[]{:S(2)}) copy-start(f32[544,768]{1,0:T(8,128)S(1)} %scatter_custom_fusion.1) | copy-start | bytes 5013508
  (109 other events, 918.8 us)
Sparse Core Ops, SparseCore 0:
  23.5 22.9 all-gather.14
  63.3 39.1 reduce-scatter.8
  104.7 37.4 all-gather.22
  144.2 37.4 all-gather.24
  191.3 29.6 all-gather.16
  259.6 60.9 reduce-scatter.10
  322.8 37.4 all-gather.26
  362.4 37.4 all-gather.28
  415.6 29.6 all-gather.18
  505.3 39.1 reduce-scatter.12
  568.9 20.2 all-gather.20
  592.3 47.8 reduce-scatter.18
  643.3 47.8 reduce-scatter.16
  693.7 47.8 reduce-scatter.22
  744.0 47.8 reduce-scatter.20
  795.0 28.7 reduce-scatter.14
  829.2 237.3 all-reduce.8
where the time goes:
time: 1090 us; the launch traced here: 1080 us
  waiting for transfers between devices  626 us (57%)
  matrix products  193 us (18%)
  blocking collectives  87.3 us (8%)
  other arithmetic  80 us (7%)
  local copies, waits for them, and re-layouts  77.9 us (7%)
  between operations  16.4 us (2%)
    psum x1, waiting for transfers between devices, body(): lax.psum(qkv_part.astype(jnp.bfloat16), 'dp').astype(jnp.float32)  148 us
    reduce_scatter x2, waiting for transfers between devices, dense_back(): lax.psum_scatter(second_part.astype(jnp.bfloat16), 'tensor', scatter_dime...  97.4 us
    reduce_scatter x2, waiting for transfers between devices, attention_forward(): lax.psum_scatter(jnp.einsum('gle,ed->gld', head_out, out_weights, preferr...  80 us
    all_gather x2, waiting for transfers between devices, dense_forward(): lax.all_gather(first_weights, 'tensor', axis=1, tiled=True)  74.4 us
    all_gather x2, waiting for transfers between devices, dense_forward(): lax.all_gather(second_weights, 'tensor', axis=0, tiled=True)  64.4 us
    reduce_scatter x2, waiting for transfers between devices, dense_back(): lax.psum_scatter(first_part.astype(jnp.bfloat16), 'tensor', scatter_dimen...  49.9 us
    all_gather x2, waiting for transfers between devices, attention_forward(): gathered = lax.all_gather(normed, 'tensor', axis=0, tiled=True)  42.2 us
    psum x1, blocking collectives, body(): lax.psum((router_part, gain_part, shift_part, out_bias_part, second_bias_...  41.6 us
  transfers between devices with their start and end apart: 17, of which 14 were waited for; matrix products, arithmetic and copies ran while one was open for 14% of the time, Pallas kernels for 0%

commit v1 on v0

--- a/solution.py
+++ b/solution.py
@@ -186,11 +186,21 @@
 def dense_forward(
     inputs, gain_row, shift_row, first_weights, first_biases, second_weights, second_biases
 ):
+
+    def _define_streams(local_block, along_dim):
+        piece_next = lax.all_to_all(
+            jnp.stack(lax.axis_size("tensor") * [local_block], axis=0),
+            axis_name="tensor",
+            split_axis=0,
+            concat_axis=0,
+        )
+        return jnp.concatenate(piece_next, axis=along_dim)
+
     normalised, inv_std, normed = norm_rows(inputs, gain_row, shift_row)
     full_first, full_first_bias, full_second = (
         lax.all_gather(first_weights, "tensor", axis=1, tiled=True),
         lax.all_gather(first_biases, "tensor", axis=0, tiled=True),
-        lax.all_gather(second_weights, "tensor", axis=0, tiled=True),
+        _define_streams(second_weights, 0),
     )
     preact = (
         jnp.einsum("gld,df->glf", normed, full_first, preferred_element_type=jnp.float32)

time: 1090 us -> 1100 us (level)
  waiting for transfers between devices: 626 us -> 446 us
  blocking collectives: 87.3 us -> 254 us
    all_gather x2, blocking collectives: 11 us -> 177 us  [dense_forward(): lax.all_gather(first_biases, 'tensor', axis=0, tiled=True)]
    reduce_scatter x2, waiting for transfers between devices: 80 us -> 0.04 us  [attention_forward(): lax.psum_scatter(jnp.einsum('gle,ed->gld', head_out, out_weights, preferr...]
    all_gather x2 -> x0, waiting for transfers between devices: 64.4 us -> none  [dense_forward(): lax.all_gather(second_weights, 'tensor', axis=0, tiled=True)]
    all_gather x2, waiting for transfers between devices: 74.4 us -> 42.6 us  [dense_forward(): lax.all_gather(first_weights, 'tensor', axis=1, tiled=True)]
  transfers between devices with their start and end apart: 17 -> 17, of which waited for: 14 -> 10; matrix products, arithmetic and copies ran while one was open for 14% -> 15% of each run, Pallas kernels for 0% -> 0%
where the time goes in v1:
time: 1100 us; the launch traced here: 1090 us
  waiting for transfers between devices  446 us (41%)
  blocking collectives  254 us (23%)
  matrix products  193 us (18%)
  local copies, waits for them, and re-layouts  84.1 us (8%)
  other arithmetic  82.1 us (7%)
  between operations  16.5 us (2%)
  starting transfers between devices  11.8 us (1%)
    all_gather x2, blocking collectives, dense_forward(): lax.all_gather(first_biases, 'tensor', axis=0, tiled=True)  177 us
    psum x1, waiting for transfers between devices, body(): lax.psum(qkv_part.astype(jnp.bfloat16), 'dp').astype(jnp.float32)  145 us
    reduce_scatter x2, waiting for transfers between devices, dense_back(): lax.psum_scatter(second_part.astype(jnp.bfloat16), 'tensor', scatter_dime...  97.6 us
    reduce_scatter x2, waiting for transfers between devices, dense_back(): lax.psum_scatter(first_part.astype(jnp.bfloat16), 'tensor', scatter_dimen...  49.3 us
    all_gather x2, waiting for transfers between devices, dense_forward(): lax.all_gather(first_weights, 'tensor', axis=1, tiled=True)  42.6 us
    all_gather x2, waiting for transfers between devices, attention_forward(): gathered = lax.all_gather(normed, 'tensor', axis=0, tiled=True)  42.4 us
    psum x1, blocking collectives, body(): lax.psum((router_part, gain_part, shift_part, out_bias_part, second_bias_...  41.5 us
    reduce_scatter x2, waiting for transfers between devices, attention_back(): lax.psum_scatter(jnp.einsum('glce,cde->gld', proj_grad, qkv_weights, pref...  39.1 us
  transfers between devices with their start and end apart: 17, of which 10 were waited for; matrix products, arithmetic and copies ran while one was open for 15% of the time, Pallas kernels for 0%

profile of v1, /device:TPU:0, one launch (start us, length us, event | category | flops | bytes accessed | tf_op | source)
XLA Modules:
  0.0 1087.4 jit_solution(2093729707928713685)
XLA Ops:
  8.0 13.7 %gather_fusion = bf16[272,768]{1,0:T(8,128)(2,1)S(1)} fusion(bf16[1,544,768]{2,1,0:T(8,128)(2,1)} %param.23, s32[272]{0:T(512)S(1)} %get-tuple-element.320), kind=kCustom, calls=%fused_computation | custom fusion | bytes 837760 | tf_op jit(solution)/shard_map/gather | solution.py:276
  24.1 9.3 gather_fusion.2
  33.6 12.8 %all-gather.11.cloned.1.call-done = bf16[4,272,768]{2,1,0:T(8,128)(2,1)} async-done(((bf16[1,272,768]{2,1,0:T(8,128)(2,1)}), bf16[4,272,768]{2,1,0:T(8,128)(2,1)}) %all-gather.11.cloned.1.call-update) | async-done | bytes 1671184 | tf_op jit(solution)/shard_map/all_gather | solution.py:119
  75.6 86.8 %all-gather.1 = bf16[1,3072]{1,0:T(2,128)(2,1)S(1)} all-gather(bf16[1,768]{1,0:T(2,128)(2,1)S(1)} %get-tuple-element.434), channel_id=3, replica_groups=mesh['dp'=8,'tensor'=4] {'tensor'}, dimensions={1}, use_global_device_ids=true | all-gather | bytes 7680 | tf_op jit(solution)/shard_map/all_gather | solution.py:202
  165.2 8.9 all-gather.19.cloned.1.call-done
  189.9 29.5 %all-gather.13.cloned.1.call-done = bf16[4,544,768]{2,1,0:T(8,128)(2,1)} async-done(((bf16[1,544,768]{2,1,0:T(8,128)(2,1)}), bf16[4,544,768]{2,1,0:T(8,128)(2,1)}) %all-gather.13.cloned.1.call-update) | async-done | bytes 3342352 | tf_op jit(solution)/shard_map/all_gather | solution.py:119
  227.9 25.0 %while.53 = (s32[]{:T(128)}, bf16[4,1,544,3,64]{2,4,3,1,0:T(8,128)(2,1)}, f32[4,1,3,544]{3,2,1,0:T(4,128)S(1)}, bf16[4,1,544,3,64]{2,4,3,1,0:T(8,128)(2,1)}, s32...) while((s32[]{:T(128)}, ...), condition=%wide.region_17.18_spmd, body=%wide.region_14.17_spmd.sunk | while | flops 238331296 | bytes 12944741 | solution.py:59
  267.4 90.5 %all-gather.3 = bf16[1,3072]{1,0:T(2,128)(2,1)S(1)} all-gather(bf16[1,768]{1,0:T(2,128)(2,1)S(1)} %get-tuple-element.433), channel_id=5, replica_groups=mesh['dp'=8,'tensor'=4] {'tensor'}, dimensions={1}, use_global_device_ids=true | all-gather | bytes 7680 | tf_op jit(solution)/shard_map/all_gather | solution.py:202
  361.3 33.7 %all-gather.21.cloned.1.call-done = bf16[1,768,3072]{2,1,0:T(8,128)(2,1)} async-done(((bf16[1,768,768]{2,1,0:T(8,128)(2,1)}), bf16[1,768,3072]{2,1,0:T(8,128)(2,1)}) %all-gather.21.cloned.1.call-update) | async-done | bytes 4718608 | tf_op jit(solution)/shard_map/all_gather | solution.py:201
  395.0 8.6 multiply_convert_fusion.2
  403.6 8.4 fusion.257
  419.6 29.4 %all-gather.15.cloned.1.call-done = bf16[4,544,768]{2,1,0:T(8,128)(2,1)} async-done(((bf16[1,544,768]{2,1,0:T(8,128)(2,1)}), bf16[4,544,768]{2,1,0:T(8,128)(2,1)}) %all-gather.15.cloned.1.call-update) | async-done | bytes 3342352 | tf_op jit(solution)/shard_map/all_gather | solution.py:154
  456.4 45.8 %while.54 = (s32[]{:T(128)}, bf16[4,1,544,3,64]{2,4,3,1,0:T(8,128)(2,1)}, bf16[4,1,544,3,64]{2,4,3,1,0:T(8,128)(2,1)}, bf16[4,1,544,3,64]{2,4,3,1,0:T(8,128)(2,1...) while((s32[]{:T(128)}, ...), condition=%wide.region_25.26_spmd, body=%wide.region_23.25_spmd.sunk | while | flops 582330752 | bytes 35354008 | solution.py:59
  509.1 39.1 %reduce-scatter.13.cloned.1.call-done = bf16[1,544,768]{2,1,0:T(8,128)(2,1)} async-done(((bf16[4,544,768]{2,1,0:T(8,128)(2,1)}), bf16[1,544,768]{2,1,0:T(8,128)(2,1)}) %reduce-scatter.13.cloned.1.call-update) | async-done | bytes 835600 | tf_op jit(solution)/shard_map/reduce_scatter | solution.py:174
  572.4 7.7 convolution_convert_fusion.3
  588.5 7.6 convolution_convert_fusion.2
  611.9 13.0 %while.55 = (s32[]{:T(128)}, bf16[2,2,272,3,64]{2,4,3,1,0:T(8,128)(2,1)}, bf16[2,2,272,3,64]{2,4,3,1,0:T(8,128)(2,1)}, bf16[2,2,272,3,64]{2,4,3,1,0:T(8,128)(2,1...) while((s32[]{:T(128)}, ...), condition=%wide.region_34.35_spmd, body=%wide.region_32.34_spmd.sunk | while | flops 288762272 | bytes 28893860 | solution.py:59
  645.5 49.3 %reduce-scatter.17.cloned.1.call-done = bf16[768,768]{1,0:T(8,128)(2,1)} async-done(((bf16[768,3072]{1,0:T(8,128)(2,1)}), bf16[768,768]{1,0:T(8,128)(2,1)}) %reduce-scatter.17.cloned.1.call-update) | async-done | bytes 1179664 | tf_op jit(solution)/shard_map/reduce_scatter | solution.py:234
  698.0 47.2 %reduce-scatter.23.cloned.1.call-done = bf16[768,768]{1,0:T(8,128)(2,1)} async-done(((bf16[3072,768]{1,0:T(8,128)(2,1)}), bf16[768,768]{1,0:T(8,128)(2,1)}) %reduce-scatter.23.cloned.1.call-update) | async-done | bytes 1179664 | tf_op jit(solution)/shard_map/reduce_scatter | solution.py:240
  745.2 50.4 %reduce-scatter.21.cloned.1.call-done = bf16[768,768]{1,0:T(8,128)(2,1)} async-done(((bf16[3072,768]{1,0:T(8,128)(2,1)}), bf16[768,768]{1,0:T(8,128)(2,1)}) %reduce-scatter.21.cloned.1.call-update) | async-done | bytes 1179664 | tf_op jit(solution)/shard_map/reduce_scatter | solution.py:240
  828.2 11.3 %all-reduce.6 = (bf16[3072]{0:T(1024)(128)(2,1)}, bf16[3072]{0:T(1024)(128)(2,1)}) all-reduce(bf16[3072]{0:T(1024)(128)(2,1)} %get-tuple-element.441, bf16[3072]{0:T(1024)(128)(2,1)} %get-tuple-element.443), channel_id=13, replica_groups=mesh['dp'=8,'tensor'=4] {'tensor'}, use_global_device_ids=true, to_apply=%region_66.67.clone | all-reduce | flops 6144 | bytes 24576
  853.2 23.6 %all-reduce.4 = (bf16[2,2,192]{2,1,0:T(2,128)(2,1)S(1)}, bf16[2,768]{1,0:T(2,128)(2,1)S(1)}) all-reduce(bf16[2,2,192]{2,1,0:T(2,128)(2,1)S(1)} %pad_maximum_fusion.15, bf16[2,768]{1,0:T(2,128)(2,1)} %pad_maximum_fusion.14), channel_id=1, replica_groups=mesh['dp'=8,'tensor'=4] {'dp'}, use_global_device_ids=true, to_apply=%region_55.56 | all-reduce | flops 2304 | bytes 9216 | tf_op jit(solution)/shard_map/psum | solution.py:366
  884.3 41.5 %all-reduce.3 = (f32[768]{0:T(1024)}, f32[2,2,768]{2,1,0:T(2,128)}, f32[2,2,768]{2,1,0:T(2,128)}, f32[2,768]{1,0:T(2,128)}, f32[2,768]{1,0:T(2,128)}) all-reduce(f32[768]{0:T(1024)S(1)} %copy-done.86, f32[2,2,768]{2,1,0:T(2,128)S(1)} %pad_maximum_fusion.10, ...), channel_id=1, replica_groups=mesh['dp'=8,'tensor'=4] {'dp','tensor'}, use_global_device_ids=true, to_apply=%region_39.40 | all-reduce | flops 9984 | bytes 79872 | tf_op jit(solution)/shard_map/psum | solution.py:355
  925.8 144.6 %all-reduce.9.cloned.1.call-done = (bf16[2,3,768,192]{2,3,1,0:T(8,128)(2,1)}, bf16[2,192,768]{2,1,0:T(8,128)(2,1)}, bf16[2,768,768]{2,1,0:T(8,128)(2,1)}, bf16[2,768,768]{2,1,0:T(8,128)(2,1)}) async-done(((bf16[2,3,768,192]{2,3,1,0:T(8,128)(2,1)}, bf16[2,192,768]{2,1,0:T(8,128)(2,1)}, bf16[2,768,768]{2,1,0:T(8,128)(2,1)}, bf16[2,768,768]{2,1,0:T(8,128)(2,1)}), (bf16[2,3,768,192]{2,3,1,0:T(8,128)(2,1)}, ...) | async-done | bytes 7077904 | tf_op jit(solution)/shard_map/psum | solution.py:365
  (535 shorter events, 321.2 us)
Async XLA Ops:
  7.2 39.3 %all-gather.11.cloned.1.call-start = ((), (), s32[]{:S(2)}) async-start(), calls=%async_computation.10 | async-start | bytes 2088960 | tf_op jit(solution)/shard_map/all_gather | solution.py:119
  8.0 176.8 %copy-start.101 = (s32[272]{0:T(512)}, s32[272]{0:T(512)S(1)}, u32[]{:S(2)}) copy-start(s32[272]{0:T(512)S(1)} %get-tuple-element.321) | copy-start | bytes 3268
  21.8 141.8 %copy-start.7 = (bf16[272,768]{1,0:T(8,128)(2,1)}, bf16[272,768]{1,0:T(8,128)(2,1)S(1)}, u32[]{:S(2)}) copy-start(bf16[272,768]{1,0:T(8,128)(2,1)S(1)} %gather_fusion) | copy-start | bytes 1253380
  22.3 151.8 %copy-start.64 = (f32[768]{0:T(1024)}, f32[768]{0:T(1024)S(1)}, u32[]{:S(2)}) copy-start(f32[768]{0:T(1024)S(1)} %get-tuple-element.447) | copy-start | bytes 9220
  22.4 151.8 %copy-start.97 = (f32[768]{0:T(1024)}, f32[768]{0:T(1024)S(1)}, u32[]{:S(2)}) copy-start(f32[768]{0:T(1024)S(1)} %get-tuple-element.313) | copy-start | bytes 9220
  22.4 166.1 %copy-start.60 = (f32[768]{0:T(1024)}, f32[768]{0:T(1024)S(1)}, u32[]{:S(2)}) copy-start(f32[768]{0:T(1024)S(1)} %get-tuple-element.445) | copy-start | bytes 9220
  23.4 140.1 %reduce-scatter.9.cloned.1.call-start = ((), (), s32[]{:S(2)}) async-start(), calls=%async_computation.11 | async-start | bytes 4177920 | tf_op jit(solution)/shard_map/reduce_scatter | solution.py:133
  63.2 110.9 %all-gather.19.cloned.1.call-start = ((), (), s32[]{:S(2)}) async-start(), calls=%async_computation.22 | async-start | bytes 5898240 | tf_op jit(solution)/shard_map/all_gather | solution.py:201
  70.3 93.0 %copy-start.9 = (bf16[1,544,768]{2,1,0:T(8,128)(2,1)S(1)}, bf16[1,544,768]{2,1,0:T(8,128)(2,1)}, u32[]{:S(2)}) copy-start(bf16[1,544,768]{2,1,0:T(8,128)(2,1)} %param.23) | copy-start | bytes 2506756
  70.3 109.9 %all-to-all-start = ((bf16[4,768,768]{2,1,0:T(8,128)(2,1)}), bf16[4,768,768]{2,1,0:T(8,128)(2,1)}, u32[]{:S(2)}, u32[]{:S(2)}) async-start(bf16[4,768,768]{2,1,0:T(8,128)(2,1)} %stack.192), calls=%async_computation.1 | async-start | bytes 9437184 | tf_op jit(solution)/shard_map/all_to_all | solution.py:191
  75.5 144.0 %all-gather.13.cloned.1.call-start = ((), (), s32[]{:S(2)}) async-start(), calls=%async_computation.12 | async-start | bytes 4177920 | tf_op jit(solution)/shard_map/all_gather | solution.py:119
  189.7 168.3 %reduce-scatter.11.cloned.1.call-start = ((), (), s32[]{:S(2)}) async-start(), calls=%async_computation.13 | async-start | bytes 8355840 | tf_op jit(solution)/shard_map/reduce_scatter | solution.py:133
  258.0 136.9 %all-gather.21.cloned.1.call-start = ((), (), s32[]{:S(2)}) async-start(), calls=%async_computation.23 | async-start | bytes 5898240 | tf_op jit(solution)/shard_map/all_gather | solution.py:201
  262.4 141.2 %all-to-all-start.1 = ((bf16[4,768,768]{2,1,0:T(8,128)(2,1)}), bf16[4,768,768]{2,1,0:T(8,128)(2,1)}, u32[]{:S(2)}, u32[]{:S(2)}) async-start(bf16[4,768,768]{2,1,0:T(8,128)(2,1)} %stack.193), calls=%async_computation.3 | async-start | bytes 9437184 | tf_op jit(solution)/shard_map/all_to_all | solution.py:191
  267.4 181.6 %all-gather.15.cloned.1.call-start = ((), (), s32[]{:S(2)}) async-start(), calls=%async_computation.14 | async-start | bytes 4177920 | tf_op jit(solution)/shard_map/all_gather | solution.py:154
  419.2 129.0 %reduce-scatter.13.cloned.1.call-start = ((), (), s32[]{:S(2)}) async-start(), calls=%async_computation.15 | async-start | bytes 4177920 | tf_op jit(solution)/shard_map/reduce_scatter | solution.py:174
  508.9 94.7 %all-gather.17.cloned.1.call-start = ((), (), s32[]{:S(2)}) async-start(), calls=%async_computation.16 | async-start | bytes 2088960 | tf_op jit(solution)/shard_map/all_gather | solution.py:154
  572.4 73.1 %reduce-scatter.19.cloned.1.call-start = ((), (), s32[]{:S(2)}) async-start(), calls=%async_computation.19 | async-start | bytes 5898240 | tf_op jit(solution)/shard_map/reduce_scatter | solution.py:234
  580.2 114.6 %reduce-scatter.17.cloned.1.call-start = ((), (), s32[]{:S(2)}) async-start(), calls=%async_computation.18 | async-start | bytes 5898240 | tf_op jit(solution)/shard_map/reduce_scatter | solution.py:234
  587.3 157.9 %reduce-scatter.23.cloned.1.call-start = ((), (), s32[]{:S(2)}) async-start(), calls=%async_computation.21 | async-start | bytes 5898240 | tf_op jit(solution)/shard_map/reduce_scatter | solution.py:240
  596.1 199.5 %reduce-scatter.21.cloned.1.call-start = ((), (), s32[]{:S(2)}) async-start(), calls=%async_computation.20 | async-start | bytes 5898240 | tf_op jit(solution)/shard_map/reduce_scatter | solution.py:240
  603.5 274.4 %reduce-scatter.15.cloned.1.call-start = ((), (), s32[]{:S(2)}) async-start(), calls=%async_computation.17 | async-start | bytes 2088960 | tf_op jit(solution)/shard_map/reduce_scatter | solution.py:174
  633.8 436.6 %all-reduce.9.cloned.1.call-start = ((), (), s32[]{:S(2)}) async-start(), calls=%async_computation.24 | async-start | bytes 14155776 | tf_op jit(solution)/shard_map/psum | solution.py:365
  884.2 190.0 %copy-start.4 = (f32[544,768]{1,0:T(8,128)}, f32[544,768]{1,0:T(8,128)S(1)}, u32[]{:S(2)}) copy-start(f32[544,768]{1,0:T(8,128)S(1)} %scatter_custom_fusion.1) | copy-start | bytes 5013508
  (113 other events, 1324.9 us)
Sparse Core Ops, SparseCore 0:
  23.5 22.9 all-gather.10
  63.3 57.1 reduce-scatter.8
  122.7 51.3 all-gather.18
  189.8 29.6 all-gather.12
  258.2 97.2 reduce-scatter.10
  357.5 37.4 all-gather.20
  419.3 29.6 all-gather.14
  509.0 39.1 reduce-scatter.12
  572.5 20.2 all-gather.16
  595.9 47.8 reduce-scatter.18
  646.9 47.8 reduce-scatter.16
  697.3 47.8 reduce-scatter.22
  747.8 47.8 reduce-scatter.20
  798.8 28.7 reduce-scatter.14
  833.0 237.4 all-reduce.8
